TPU v7x, 32 devices: a whole 2x2x4 slice. The times are simulated.
32 devices in a mesh: dp: 2 (over y), seq: 8 (over z, x), tensor: 2 (over core).
Axes of the slice: x: 2, y: 2, z: 4, core: 2. Of those that a mesh axis runs over, the one named last changes fastest.
Arguments:
- tokens: bfloat16 [4, 8192, 512], P('dp', 'seq'), may hold values from -6 to 6
- segments: int32 [4, 8192], P('dp', 'seq'), may hold values from 0 to 15, never falling along the last dimension, each value on 1 to 5120 neighbouring positions
- keep_mask: int32 [4, 8192], P('dp', 'seq'), may hold values 0 or 1
- cotangent: bfloat16 [4, 8192, 512], P('dp', 'seq'), may hold values from -6 to 6
- ln1_gain: float32 [512], replicated, may hold values from 0.25 to 1.75
- ln1_bias: float32 [512], replicated, may hold values from -1.5 to 1.5
- w_qkv: bfloat16 [3, 512, 512], P(None, None, 'tensor'), may hold values from -0.25 to 0.25
- qv_bias: float32 [2, 512], P(None, 'tensor'), may hold values from -1.5 to 1.5
- w_out: bfloat16 [512, 512], P('tensor'), may hold values from -1.5 to 1.5
- b_out: float32 [512], replicated, may hold values from -1.5 to 1.5
- ln2_gain: float32 [512], replicated, may hold values from 0.25 to 1.75
- ln2_bias: float32 [512], replicated, may hold values from -1.5 to 1.5
- w_fc: bfloat16 [512, 2048], P(None, 'tensor'), may hold values from -0.25 to 0.25
- b_fc: float32 [2048], P('tensor'), may hold values from -1.5 to 1.5
- w_proj: bfloat16 [2048, 512], P('tensor'), may hold values from -0.125 to 0.125
- b_proj: float32 [512], replicated, may hold values from -1.5 to 1.5
Outputs:
- layer_out: bfloat16 [4, 8192, 512], P('dp', 'seq')
- grad_tokens: bfloat16 [4, 8192, 512], P('dp', 'seq')
- grad_ln1_gain: float32 [512], replicated
- grad_ln1_bias: float32 [512], replicated
- grad_w_qkv: float32 [3, 512, 512], P(None, None, 'tensor')
- grad_qv_bias: float32 [2, 512], P(None, 'tensor')
- grad_w_out: float32 [512, 512], P('tensor')
- grad_b_out: float32 [512], replicated
- grad_ln2_gain: float32 [512], replicated
- grad_ln2_bias: float32 [512], replicated
- grad_w_fc: float32 [512, 2048], P(None, 'tensor')
- grad_b_fc: float32 [2048], P('tensor')
- grad_w_proj: float32 [2048, 512], P('tensor')
- grad_b_proj: float32 [512], replicated
Inputs may be any that keep to these rules, and one draw needn't show every extreme that they name: `segments`: in each sequence the document numbers never fall; each document holds 1 to 5120 tokens, and one holds exactly 5120.
All inputs are finite; a program needn't handle non-finite values. No bound on the sum of `keep_mask` on one device may be relied on, other than what follows from the above.
Results may differ from a plain program's by a relative error of at most 0.024.
Values may be sent and summed in bfloat16 or wider, within the bound.
No kernel may reach another device: no remote copies, remote signals or barrier semaphores. Data moves between devices by JAX's collectives and lax.ppermute only.
A program may use at most 512 MiB of HBM per device.

v0:
```python
import jax
import jax.numpy as jnp
from jax import lax
from jax.sharding import PartitionSpec as P

HEAD_DIM = 64
EPSILON = 1e-05
MASKED = -1e30


def layer_norm(rows, gain, offset):
    centred = rows - jnp.mean(rows, -1, keepdims=True)
    rstd = lax.rsqrt(jnp.mean(centred * centred, -1, keepdims=True) + EPSILON)
    normed = centred * rstd
    return (normed * gain + offset, normed, rstd)


def norm_back(grad_norm, normed, rstd, gain):
    scaled = grad_norm * gain
    return rstd * (
        scaled
        - jnp.mean(scaled, -1, keepdims=True)
        - normed * jnp.mean(scaled * normed, -1, keepdims=True)
    )


def gelu_parts(pre_act):
    sigma = jax.nn.sigmoid(1.702 * pre_act)
    return (pre_act * sigma, sigma + 1.702 * pre_act * sigma * (1.0 - sigma))


def visible(query_pos, query_seg, key_pos, key_seg, key_keep):
    allowed = (query_seg[:, None] == key_seg[None, :]) & (key_pos[None, :] <= query_pos[:, None])
    return allowed & ((key_keep[None, :] == 1) | (key_pos[None, :] == query_pos[:, None]))


def on_device(
    tokens,
    segments,
    keep_mask,
    cotangent,
    ln1_gain,
    ln1_bias,
    w_qkv,
    qv_bias,
    w_out,
    b_out,
    ln2_gain,
    ln2_bias,
    w_fc,
    b_fc,
    w_proj,
    b_proj,
):
    sequences, group_rows, width = tokens.shape
    local_width = w_qkv.shape[2]
    heads_here = local_width // HEAD_DIM
    score_scale = HEAD_DIM ** (-0.5)
    seg_all, keep_all = (
        lax.all_gather(segments, "seq", axis=1, tiled=True),
        lax.all_gather(keep_mask, "seq", axis=1, tiled=True),
    )
    full_length = seg_all.shape[1]
    key_block = min(512, full_length)
    block_count = full_length // key_block
    piece_index = lax.axis_index("seq")
    query_pos = piece_index * group_rows + jnp.arange(group_rows, dtype=jnp.int32)
    params = (
        ln1_gain,
        ln1_bias,
        w_qkv,
        qv_bias,
        w_out,
        b_out,
        ln2_gain,
        ln2_bias,
        w_fc,
        b_fc,
        w_proj,
        b_proj,
    )
    sums = [jnp.zeros(p.shape, jnp.float32) for p in params]
    outputs = []
    input_grads = []
    for sequence_index in range(sequences):
        rows = tokens[sequence_index].astype(jnp.float32)
        seg_row = seg_all[sequence_index]
        keep_row = keep_all[sequence_index]
        query_seg = segments[sequence_index]
        normed_one_out, normed_one, rstd_one = layer_norm(rows, ln1_gain, ln1_bias)
        hidden_one = normed_one_out.astype(jnp.bfloat16)
        projected = jnp.einsum("te,ced->ctd", hidden_one, w_qkv, preferred_element_type=jnp.float32)
        queries = (projected[0] + qv_bias[0]).astype(jnp.bfloat16)
        keys = projected[1].astype(jnp.bfloat16)
        values = (projected[2] + qv_bias[1]).astype(jnp.bfloat16)
        query_heads = queries.reshape(group_rows, heads_here, HEAD_DIM)
        best = jnp.full((heads_here, group_rows), MASKED, jnp.float32)
        key_part = lax.all_gather(keys, "seq", axis=0, tiled=True)
        value_part = lax.all_gather(values, "seq", axis=0, tiled=True)
        row_count = key_part.shape[0]
        key_pos = jnp.arange(row_count, dtype=jnp.int32)
        key_seg = seg_row
        key_keep = keep_row
        allowed = visible(query_pos, query_seg, key_pos, key_seg, key_keep)[None]
        scores = (
            jnp.einsum(
                "qhd,khd->hqk",
                query_heads,
                key_part.reshape(row_count, heads_here, HEAD_DIM),
                preferred_element_type=jnp.float32,
            )
            * score_scale
        )
        scores = jnp.where(allowed, scores, MASKED)
        new_best = jnp.maximum(best, jnp.max(scores, -1))
        weights = jnp.where(allowed, jnp.exp(scores - new_best[..., None]), 0.0)
        weight_sum = jnp.sum(weights, -1)
        accum = jnp.einsum(
            "hqk,khd->hqd",
            weights.astype(jnp.bfloat16),
            value_part.reshape(row_count, heads_here, HEAD_DIM),
            preferred_element_type=jnp.float32,
        )
        best, weight_sum, accum = (new_best, weight_sum, accum)
        log_sum = best + jnp.log(weight_sum)
        attn_out = (
            (accum / weight_sum[..., None])
            .transpose(1, 0, 2)
            .reshape(group_rows, local_width)
            .astype(jnp.bfloat16)
        )
        attn_term = jnp.dot(attn_out, w_out, preferred_element_type=jnp.float32)
        middle = (
            rows + lax.psum(attn_term.astype(jnp.bfloat16), "tensor").astype(jnp.float32) + b_out
        )
        normed_two_out, normed_two, rstd_two = layer_norm(middle, ln2_gain, ln2_bias)
        hidden_two = normed_two_out.astype(jnp.bfloat16)
        pre_act = jnp.dot(hidden_two, w_fc, preferred_element_type=jnp.float32) + b_fc
        activated, slope = gelu_parts(pre_act)
        act_low = activated.astype(jnp.bfloat16)
        feed_term = jnp.dot(act_low, w_proj, preferred_element_type=jnp.float32)
        feed = lax.psum(feed_term.astype(jnp.bfloat16), "tensor").astype(jnp.float32) + b_proj
        outputs.append((middle + feed).astype(jnp.bfloat16))
        grad_out = cotangent[sequence_index]
        grad_out_wide = grad_out.astype(jnp.float32)
        sums[11] = sums[11] + jnp.sum(grad_out_wide, 0)
        sums[10] = sums[10] + jnp.einsum(
            "tf,td->fd", act_low, grad_out, preferred_element_type=jnp.float32
        )
        grad_act = jnp.einsum("td,fd->tf", grad_out, w_proj, preferred_element_type=jnp.float32)
        grad_pre = (grad_act * slope).astype(jnp.bfloat16)
        sums[9] = sums[9] + jnp.sum(grad_pre.astype(jnp.float32), 0)
        sums[8] = sums[8] + jnp.einsum(
            "te,tf->ef", hidden_two, grad_pre, preferred_element_type=jnp.float32
        )
        grad_hidden_two = lax.psum(
            jnp.einsum("tf,ef->te", grad_pre, w_fc, preferred_element_type=jnp.float32).astype(
                jnp.bfloat16
            ),
            "tensor",
        ).astype(jnp.float32)
        sums[6] = sums[6] + jnp.sum(grad_hidden_two * normed_two, 0)
        sums[7] = sums[7] + jnp.sum(grad_hidden_two, 0)
        grad_middle = grad_out_wide + norm_back(grad_hidden_two, normed_two, rstd_two, ln2_gain)
        grad_branch = grad_middle.astype(jnp.bfloat16)
        sums[5] = sums[5] + jnp.sum(grad_branch.astype(jnp.float32), 0)
        sums[4] = sums[4] + jnp.einsum(
            "tc,td->cd", attn_out, grad_branch, preferred_element_type=jnp.float32
        )
        grad_mixed = jnp.einsum(
            "td,cd->tc", grad_branch, w_out, preferred_element_type=jnp.float32
        ).astype(jnp.bfloat16)
        grad_heads = grad_mixed.reshape(group_rows, heads_here, HEAD_DIM)
        row_dot = jnp.sum(
            (grad_mixed.astype(jnp.float32) * attn_out.astype(jnp.float32)).reshape(
                group_rows, heads_here, HEAD_DIM
            ),
            -1,
        ).T
        key_use, value_use = (
            lax.all_gather(keys, "seq", axis=0, tiled=True),
            lax.all_gather(values, "seq", axis=0, tiled=True),
        )

        def make_step(key_src, value_src, seg_src, keep_src, pos_base, block_rows):

            def key_step(grad_query_sum, block_index):
                first_row = block_index * block_rows
                key_part = lax.dynamic_slice_in_dim(key_src, first_row, block_rows).reshape(
                    block_rows, heads_here, HEAD_DIM
                )
                value_part = lax.dynamic_slice_in_dim(value_src, first_row, block_rows).reshape(
                    block_rows, heads_here, HEAD_DIM
                )
                key_pos = pos_base + first_row + jnp.arange(block_rows, dtype=jnp.int32)
                key_seg = lax.dynamic_slice_in_dim(seg_src, first_row, block_rows)
                key_keep = lax.dynamic_slice_in_dim(keep_src, first_row, block_rows)
                allowed = visible(query_pos, query_seg, key_pos, key_seg, key_keep)[None]
                scores = (
                    jnp.einsum(
                        "qhd,khd->hqk", query_heads, key_part, preferred_element_type=jnp.float32
                    )
                    * score_scale
                )
                probs = jnp.where(allowed, jnp.exp(scores - log_sum[..., None]), 0.0)
                grad_probs = jnp.einsum(
                    "qhd,khd->hqk", grad_heads, value_part, preferred_element_type=jnp.float32
                )
                grad_scores = (probs * (grad_probs - row_dot[..., None])).astype(jnp.bfloat16)
                grad_query_sum = grad_query_sum + jnp.einsum(
                    "hqk,khd->qhd", grad_scores, key_part, preferred_element_type=jnp.float32
                )
                key_term = jnp.einsum(
                    "hqk,qhd->khd", grad_scores, query_heads, preferred_element_type=jnp.float32
                )
                value_term = jnp.einsum(
                    "hqk,qhd->khd",
                    probs.astype(jnp.bfloat16),
                    grad_heads,
                    preferred_element_type=jnp.float32,
                )
                return (
                    grad_query_sum,
                    (
                        key_term.reshape(block_rows, local_width),
                        value_term.reshape(block_rows, local_width),
                    ),
                )

            return key_step

        query_start = jnp.zeros((group_rows, heads_here, HEAD_DIM), jnp.float32)
        step_fn = make_step(key_use, value_use, seg_row, keep_row, 0, key_block)
        grad_query_sum, (key_terms, value_terms) = lax.scan(
            step_fn, query_start, jnp.arange(block_count, dtype=jnp.int32)
        )
        key_terms = key_terms.reshape(full_length, local_width) * score_scale
        value_terms = value_terms.reshape(full_length, local_width)
        key_grads, value_grads = (
            lax.psum_scatter(
                key_terms.astype(jnp.bfloat16), "seq", scatter_dimension=0, tiled=True
            ).astype(jnp.float32),
            lax.psum_scatter(
                value_terms.astype(jnp.bfloat16), "seq", scatter_dimension=0, tiled=True
            ).astype(jnp.float32),
        )
        grad_queries = (
            (grad_query_sum * score_scale).reshape(group_rows, local_width).astype(jnp.bfloat16)
        )
        value_low = value_grads.astype(jnp.bfloat16)
        stacked = jnp.stack([grad_queries, key_grads.astype(jnp.bfloat16), value_low])
        sums[2] = sums[2] + jnp.einsum(
            "te,ctd->ced", hidden_one, stacked, preferred_element_type=jnp.float32
        )
        sums[3] = sums[3] + jnp.stack(
            [
                jnp.sum(grad_queries.astype(jnp.float32), 0),
                jnp.sum(value_low.astype(jnp.float32), 0),
            ]
        )
        grad_hidden_one = lax.psum(
            jnp.einsum("ctd,ced->te", stacked, w_qkv, preferred_element_type=jnp.float32).astype(
                jnp.bfloat16
            ),
            "tensor",
        ).astype(jnp.float32)
        sums[0] = sums[0] + jnp.sum(grad_hidden_one * normed_one, 0)
        sums[1] = sums[1] + jnp.sum(grad_hidden_one, 0)
        grad_rows = grad_middle + norm_back(grad_hidden_one, normed_one, rstd_one, ln1_gain)
        input_grads.append(grad_rows.astype(jnp.bfloat16))
    totals = (
        lax.psum(sums[0].astype(jnp.bfloat16), ("dp", "seq")).astype(jnp.float32),
        lax.psum(sums[1].astype(jnp.bfloat16), ("dp", "seq")).astype(jnp.float32),
        lax.psum(sums[2].astype(jnp.bfloat16), ("dp", "seq")).astype(jnp.float32),
        lax.psum(sums[3].astype(jnp.bfloat16), ("dp", "seq")).astype(jnp.float32),
        lax.psum(sums[4].astype(jnp.bfloat16), ("dp", "seq")).astype(jnp.float32),
        lax.psum(sums[5].astype(jnp.bfloat16), ("dp", "seq")).astype(jnp.float32),
        lax.psum(sums[6].astype(jnp.bfloat16), ("dp", "seq")).astype(jnp.float32),
        lax.psum(sums[7].astype(jnp.bfloat16), ("dp", "seq")).astype(jnp.float32),
        lax.psum(sums[8].astype(jnp.bfloat16), ("dp", "seq")).astype(jnp.float32),
        lax.psum(sums[9].astype(jnp.bfloat16), ("dp", "seq")).astype(jnp.float32),
        lax.psum(sums[10].astype(jnp.bfloat16), ("dp", "seq")).astype(jnp.float32),
        lax.psum(sums[11].astype(jnp.bfloat16), ("dp", "seq")).astype(jnp.float32),
    )
    return (
        jnp.stack(outputs),
        jnp.stack(input_grads),
        totals[0],
        totals[1],
        totals[2],
        totals[3],
        totals[4],
        totals[5],
        totals[6],
        totals[7],
        totals[8],
        totals[9],
        totals[10],
        totals[11],
    )


def solution(mesh):
    return jax.shard_map(
        on_device,
        mesh=mesh,
        in_specs=(
            P("dp", "seq", None),
            P("dp", "seq"),
            P("dp", "seq"),
            P("dp", "seq", None),
            P(),
            P(),
            P(None, None, "tensor"),
            P(None, "tensor"),
            P("tensor", None),
            P(),
            P(),
            P(),
            P(None, "tensor"),
            P("tensor"),
            P("tensor", None),
            P(),
        ),
        out_specs=(
            P("dp", "seq", None),
            P("dp", "seq", None),
            P(),
            P(),
            P(None, None, "tensor"),
            P(None, "tensor"),
            P("tensor", None),
            P(),
            P(),
            P(),
            P(None, "tensor"),
            P("tensor"),
            P("tensor", None),
            P(),
        ),
        check_vma=False,
    )
```

profile of v0, /device:TPU:0, one launch (start us, length us, event | category | flops | bytes accessed | tf_op | source)
XLA Modules:
  0.0 1566.7 jit_solution(10269686080167025364)
XLA Ops:
  23.1 32.7 %all_gather.22 = s32[2,8192]{1,0:T(2,128)S(1)} all-gather(s32[2,1024]{1,0:T(2,128)S(1)} %copy-done.84), channel_id=1, replica_groups=mesh['dp'=2,'seq'=8,'tensor'=2] {'seq'}, dimensions={1}, use_global_device_ids=true | all-gather | bytes 73728 | tf_op jit(solution)/shard_map/all_gather | solution.py:60
  58.3 31.5 %all_gather.23 = s32[2,8192]{1,0:T(2,128)S(1)} all-gather(s32[2,1024]{1,0:T(2,128)S(1)} %copy-done.89), channel_id=1, replica_groups=mesh['dp'=2,'seq'=8,'tensor'=2] {'seq'}, dimensions={1}, use_global_device_ids=true | all-gather | bytes 73728 | tf_op jit(solution)/shard_map/all_gather | solution.py:61
  92.1 24.5 %fusion.37 = (pred[1024,8192]{1,0:T(8,128)(4,1)}, pred[1024,8192]{1,0:T(8,128)(4,1)}) fusion(s32[8192]{0:T(1024)S(1)} %bitcast.455, s32[1024]{0:T(1024)S(1)} %iota_add_fusion.4, s32[1024]{0:T(1024)S(1)} %bitcast.451, pred[8192]{0:T(1024)(128)(4,1)S(1)} %get-tuple-element.339, pred[8192]{0:T(1024)(128)(4,1)S(1)} %get-tuple-element.338, ...), kind=kLoop, calls=%fused_computation.59 | loop fusion | flops 83886080 | bytes 16871424 | tf_op jit(solution)/shard_map/and | solution.py:34
  116.7 50.0 %fusion.20 = (f32[4,1024]{1,0:T(4,128)S(1)}, f32[4,1024,8192]{2,1,0:T(8,128)}) fusion(pred[1024,8192]{1,0:T(8,128)(4,1)} %get-tuple-element.451, bf16[1024,4,64]{0,2,1:T(8,128)(2,1)S(1)} %get-tuple-element.729, bf16[8192,4,64]{0,2,1:T(8,128)(2,1)} %bitcast.448), kind=kOutput, calls=%fused_computation.42 | convolution fusion | flops 4395626496 | bytes 147341312 | tf_op jit(solution)/shard_map/qhd,khd->hqk/dot_general | solution.py:106
  166.8 50.2 %fusion.21 = (f32[4,1024]{1,0:T(4,128)S(1)}, f32[4,1024,8192]{2,1,0:T(8,128)}) fusion(pred[1024,8192]{1,0:T(8,128)(4,1)} %get-tuple-element.450, bf16[1024,4,64]{0,2,1:T(8,128)(2,1)S(1)} %get-tuple-element.672, bf16[8192,4,64]{0,2,1:T(8,128)(2,1)} %bitcast.445), kind=kOutput, calls=%fused_computation.43 | convolution fusion | flops 4395626496 | bytes 147341312 | tf_op jit(solution)/shard_map/qhd,khd->hqk/dot_general | solution.py:106
  217.6 44.0 %fusion.22 = f32[4,1024]{1,0:T(4,128)S(1)} fusion(f32[4,1024,8192]{2,1,0:T(8,128)} %get-tuple-element.459, f32[4,1024]{1,0:T(4,128)S(1)} %broadcast_maximum_fusion.1, pred[1024,8192]{1,0:T(8,128)(4,1)} %get-tuple-element.451), kind=kLoop, calls=%fused_computation.44 | loop fusion | flops 167768064 | bytes 142639104 | tf_op jit(solution)/shard_map/reduce_sum | solution.py:117
  261.7 51.2 %divide_convert_fusion.1 = bf16[1024,4,64]{0,2,1:T(8,128)(2,1)S(1)} fusion(bf16[8192,4,64]{0,2,1:T(8,128)(2,1)} %bitcast.450, f32[4,1024,8192]{2,1,0:T(8,128)} %get-tuple-element.459, f32[4,1024]{1,0:T(4,128)S(1)} %broadcast_maximum_fusion.1, pred[1024,8192]{1,0:T(8,128)(4,1)} %get-tuple-element.451, f32[1024,4]{0,1:T(4,128)S(1)} %bitcast.460), kind=kOutput, calls=%fused_computation.207 | convolution fusion | flops 4463263744 | bytes 147357696 | tf_op jit(solution)/shard_map/hqk,khd->hqd/dot_general | solution.py:118
  314.3 43.9 %fusion.24 = f32[4,1024]{1,0:T(4,128)S(1)} fusion(f32[4,1024,8192]{2,1,0:T(8,128)} %get-tuple-element.461, f32[4,1024]{1,0:T(4,128)S(1)} %broadcast_maximum_fusion, pred[1024,8192]{1,0:T(8,128)(4,1)} %get-tuple-element.450), kind=kLoop, calls=%fused_computation.46 | loop fusion | flops 167768064 | bytes 142639104 | tf_op jit(solution)/shard_map/reduce_sum | solution.py:117
  358.2 51.0 %divide_convert_fusion = bf16[1024,4,64]{0,2,1:T(8,128)(2,1)} fusion(bf16[8192,4,64]{0,2,1:T(8,128)(2,1)} %bitcast.447, f32[4,1024,8192]{2,1,0:T(8,128)} %get-tuple-element.461, f32[4,1024]{1,0:T(4,128)S(1)} %broadcast_maximum_fusion, pred[1024,8192]{1,0:T(8,128)(4,1)} %get-tuple-element.450, f32[1024,4]{0,1:T(4,128)S(1)} %bitcast.459), kind=kOutput, calls=%fused_computation.205 | convolution fusion | flops 4463263744 | bytes 147357696 | tf_op jit(solution)/shard_map/hqk,khd->hqd/dot_general | solution.py:118
  412.2 21.7 %all-reduce.16.cloned.1.call-done = (bf16[1024,512]{1,0:T(8,128)(2,1)}, bf16[1024,512]{1,0:T(8,128)(2,1)}) async-done(((bf16[1024,512]{1,0:T(8,128)(2,1)}, bf16[1024,512]{1,0:T(8,128)(2,1)}), (bf16[1024,512]{1,0:T(8,128)(2,1)}, bf16[1024,512]{1,0:T(8,128)(2,1)})) %all-reduce.16.cloned.1.call-update) | async-done | bytes 2097168 | tf_op jit(solution)/shard_map/psum | solution.py:134
  439.4 5.0 multiply_convert_fusion.5
  458.0 4.6 copy.97
  462.7 15.1 all-reduce.14.cloned.1.call-done
  477.8 5.1 fusion.86
  493.0 300.7 %while.30 = (s32[]{:T(128)}, f32[1024,4,64]{0,2,1:T(8,128)S(1)}, f32[16,512,256]{1,2,0:T(8,128)}, bf16[16,512,256]{1,2,0:T(8,128)(2,1)}, s32[16]{0:T(128)S(1)}, ...) while((s32[]{:T(128)}, f32[1024,4,64]{0,2,1:T(8,128)S(1)}, ...), condition=%wide.region_21.22_spmd.clone, body=%wide.region_20.21_spmd.clone.sunk | while | flops 1366820864 | bytes 135865776 | solution.py:234
  498.3 4.6 fusion.248
  517.2 4.6 fusion.248
  611.1 4.6 fusion.248
  648.7 4.6 fusion.248
  793.7 6.9 copy.56
  801.3 6.6 multiply_convert_fusion.1
  808.0 6.3 copy.55
  821.6 302.6 %while.31 = (s32[]{:T(128)}, f32[1024,4,64]{0,2,1:T(8,128)S(1)}, f32[16,512,256]{1,2,0:T(8,128)}, bf16[16,512,256]{1,2,0:T(8,128)(2,1)}, s32[16]{0:T(128)S(1)}, ...) while((s32[]{:T(128)}, f32[1024,4,64]{0,2,1:T(8,128)S(1)}, ...), condition=%wide.region_32.33_spmd.clone, body=%wide.region_31.32_spmd.clone.sunk | while | flops 1366820864 | bytes 135865776 | solution.py:234
  826.9 4.7 fusion.263
  845.9 4.7 fusion.263
  865.0 4.7 fusion.263
  883.9 4.7 fusion.263
  902.8 4.7 fusion.263
  921.8 4.7 fusion.263
  940.8 4.7 fusion.263
  959.8 4.7 fusion.263
  978.7 4.7 fusion.263
  997.6 4.7 fusion.263
  1016.5 4.7 fusion.263
  1035.3 4.7 fusion.263
  1054.1 4.7 fusion.263
  1073.0 4.7 fusion.263
  1091.8 4.7 fusion.263
  1110.6 4.7 fusion.263
  1124.2 6.8 copy.59
  1131.1 6.6 multiply_convert_fusion
  1137.7 6.4 copy.58
  1170.8 49.7 %reduce-scatter.11.cloned.1.call-done = bf16[1024,256]{1,0:T(8,128)(2,1)} async-done(((bf16[8192,256]{1,0:T(8,128)(2,1)}), bf16[1024,256]{1,0:T(8,128)(2,1)}) %reduce-scatter.11.cloned.1.call-update) | async-done | bytes 524304 | tf_op jit(solution)/shard_map/reduce_scatter | solution.py:243
  1220.4 91.7 %reduce-scatter.9.cloned.1.call-done = bf16[1024,256]{1,0:T(8,128)(2,1)} async-done(((bf16[8192,256]{1,0:T(8,128)(2,1)}), bf16[1024,256]{1,0:T(8,128)(2,1)}) %reduce-scatter.9.cloned.1.call-update) | async-done | bytes 524304 | tf_op jit(solution)/shard_map/reduce_scatter | solution.py:240
  1331.9 134.7 %all-reduce.10.cloned.1.call-done = (bf16[3,512,256]{1,2,0:T(8,128)(2,1)}, bf16[256,512]{1,0:T(8,128)(2,1)}, bf16[512,1024]{1,0:T(8,128)(2,1)}, bf16[1024,512]{1,0:T(8,128)(2,1)}) async-done(((bf16[3,512,256]{1,2,0:T(8,128)(2,1)}, bf16[256,512]{1,0:T(8,128)(2,1)}, bf16[512,1024]{1,0:T(8,128)(2,1)}, bf16[1024,512]{1,0:T(8,128)(2,1)}), (bf16[3,512,256]{1,2,0:T(8,128)(2,1)}, bf16[256,512]{1,0:T(8,128)(2,1)}, ...) | async-done | bytes 3145744 | tf_op jit(solution)/shard_map/psum | solution.py:274
  1474.4 23.3 %all-reduce.12.cloned.1.call-done = (bf16[1024,512]{1,0:T(8,128)(2,1)}, bf16[1024,512]{1,0:T(8,128)(2,1)}, bf16[1024,512]{1,0:T(8,128)(2,1)}, bf16[1024,512]{1,0:T(8,128)(2,1)}) async-done(((bf16[1024,512]{1,0:T(8,128)(2,1)}, bf16[1024,512]{1,0:T(8,128)(2,1)}, bf16[1024,512]{1,0:T(8,128)(2,1)}, bf16[1024,512]{1,0:T(8,128)(2,1)}), (bf16[1024,512]{1,0:T(8,128)(2,1)}, bf16[1024,512]{1,0:T(8,128)(2,1)}, ...) | async-done | bytes 4194320 | tf_op jit(solution)/shard_map/psum | solution.py:142
  1497.7 6.0 fusion.87
  1503.8 42.9 %all-reduce = (bf16[512]{0:T(512)(128)(2,1)S(1)}, bf16[512]{0:T(512)(128)(2,1)S(1)}, bf16[2,256]{1,0:T(2,128)(2,1)S(1)}, bf16[512]{0:T(512)(128)(2,1)S(1)}, bf16...) all-reduce(bf16[512]{0:T(512)(128)(2,1)S(1)} %add_convert_fusion.15, ...), channel_id=1, replica_groups=mesh['dp'=2,'seq'=8,'tensor'=2] {'dp','seq'}, use_global_device_ids=true, to_apply=%region_40.41 | all-reduce | flops 4608 | bytes 18432 | tf_op jit(solution)/shard_map/psum | solution.py:272
  (1092 shorter events, 616.6 us)
Async XLA Ops:
  7.2 430.6 %copy-start = (bf16[512,1024]{1,0:T(8,128)(2,1)S(1)}, bf16[512,1024]{1,0:T(8,128)(2,1)}, u32[]{:S(2)}) copy-start(bf16[512,1024]{1,0:T(8,128)(2,1)} %param.32) | copy-start | bytes 3145732
  7.2 109.5 %all-gather.11.cloned.1.call-start = ((), (), s32[]{:S(2)}) async-start(), calls=%async_computation.10 | async-start | bytes 4718592 | tf_op jit(solution)/shard_map/all_gather | solution.py:98
  14.5 152.3 %all-gather.13.cloned.1.call-start = ((), (), s32[]{:S(2)}) async-start(), calls=%async_computation.11 | async-start | bytes 4718592 | tf_op jit(solution)/shard_map/all_gather | solution.py:98
  19.6 242.0 %all-gather.7.cloned.1.call-start = ((), (), s32[]{:S(2)}) async-start(), calls=%async_computation.4 | async-start | bytes 4718592 | tf_op jit(solution)/shard_map/all_gather | solution.py:99
  22.4 335.8 %all-gather.9.cloned.1.call-start = ((), (), s32[]{:S(2)}) async-start(), calls=%async_computation.5 | async-start | bytes 4718592 | tf_op jit(solution)/shard_map/all_gather | solution.py:99
  23.0 410.8 %all-reduce.16.cloned.1.call-start = ((), (), s32[]{:S(2)}) async-start(), calls=%async_computation.15 | async-start | bytes 4194304 | tf_op jit(solution)/shard_map/psum | solution.py:134
  55.8 36.3 %copy-start.54 = (s32[1,1024]{1,0:T(1,128)}, s32[1,1024]{1,0:T(1,128)S(1)}, u32[]{:S(2)}) copy-start(s32[1,1024]{1,0:T(1,128)S(1)} %get-tuple-element.669) | copy-start | bytes 12292
  55.8 36.3 %copy-start.56 = (s32[1,1024]{1,0:T(1,128)}, s32[1,1024]{1,0:T(1,128)S(1)}, u32[]{:S(2)}) copy-start(s32[1,1024]{1,0:T(1,128)S(1)} %get-tuple-element.726) | copy-start | bytes 12292
  55.8 34.9 %slice-start = ((f32[3,1024,256]{1,2,0:T(8,128)}), f32[1,1024,256]{1,2,0:T(8,128)S(1)}, s32[]{:S(2)}) async-start(f32[3,1024,256]{1,2,0:T(8,128)} %copy-done.36), calls=%async_computation.16 | async-start | bytes 2097152 | tf_op jit(solution)/shard_map/slice | solution.py:93
  58.3 58.4 %copy-start.58 = (s32[1,8192]{1,0:T(1,128)}, s32[1,8192]{1,0:T(1,128)S(1)}, u32[]{:S(2)}) copy-start(s32[1,8192]{1,0:T(1,128)S(1)} %get-tuple-element.444) | copy-start | bytes 98308
  58.3 58.4 %copy-start.59 = (s32[1,8192]{1,0:T(1,128)}, s32[1,8192]{1,0:T(1,128)S(1)}, u32[]{:S(2)}) copy-start(s32[1,8192]{1,0:T(1,128)S(1)} %get-tuple-element.445) | copy-start | bytes 98308
  92.1 24.6 %copy-start.16 = (bf16[1024,4,64]{0,2,1:T(8,128)(2,1)}, bf16[1024,4,64]{0,2,1:T(8,128)(2,1)S(1)}, u32[]{:S(2)}) copy-start(bf16[1024,4,64]{0,2,1:T(8,128)(2,1)S(1)} %get-tuple-element.729) | copy-start | bytes 1572868
  92.1 74.7 %copy-start.14 = (bf16[1024,4,64]{0,2,1:T(8,128)(2,1)}, bf16[1024,4,64]{0,2,1:T(8,128)(2,1)S(1)}, u32[]{:S(2)}) copy-start(bf16[1024,4,64]{0,2,1:T(8,128)(2,1)S(1)} %get-tuple-element.672) | copy-start | bytes 1572868
  166.7 50.3 %copy-start.68 = (f32[4,1024]{1,0:T(4,128)}, f32[4,1024]{1,0:T(4,128)S(1)}, u32[]{:S(2)}) copy-start(f32[4,1024]{1,0:T(4,128)S(1)} %get-tuple-element.458) | copy-start | bytes 49156
  261.6 51.2 %copy-start.64 = (f32[4,1024]{1,0:T(4,128)}, f32[4,1024]{1,0:T(4,128)S(1)}, u32[]{:S(2)}) copy-start(f32[4,1024]{1,0:T(4,128)S(1)} %fusion.22) | copy-start | bytes 49156
  261.7 51.2 %copy-start.37 = (bf16[256,512]{1,0:T(8,128)(2,1)S(1)}, bf16[256,512]{1,0:T(8,128)(2,1)}, u32[]{:S(2)}) copy-start(bf16[256,512]{1,0:T(8,128)(2,1)} %param.28) | copy-start | bytes 786436
  312.8 45.4 %copy-start.32 = (bf16[1024,4,64]{0,2,1:T(8,128)(2,1)}, bf16[1024,4,64]{0,2,1:T(8,128)(2,1)S(1)}, u32[]{:S(2)}) copy-start(bf16[1024,4,64]{0,2,1:T(8,128)(2,1)S(1)} %divide_convert_fusion.1) | copy-start | bytes 1572868
  409.2 24.6 %copy-start.8 = (bf16[2,1024,512]{2,1,0:T(8,128)(2,1)S(1)}, bf16[2,1024,512]{2,1,0:T(8,128)(2,1)}, u32[]{:S(2)}) copy-start(bf16[2,1024,512]{2,1,0:T(8,128)(2,1)} %param.20) | copy-start | bytes 6291460
  409.2 24.6 %copy-start.74 = (f32[512]{0:T(512)S(1)}, f32[512]{0:T(512)}, u32[]{:S(2)}) copy-start(f32[512]{0:T(512)} %param.29) | copy-start | bytes 6148
  411.9 65.9 %all-reduce.14.cloned.1.call-start = ((), (), s32[]{:S(2)}) async-start(), calls=%async_computation.14 | async-start | bytes 4194304 | tf_op jit(solution)/shard_map/psum | solution.py:156
  436.3 46.7 %copy-start.72 = (f32[1024]{0:T(1024)}, f32[1024]{0:T(1024)S(1)}, u32[]{:S(2)}) copy-start(f32[1024]{0:T(1024)S(1)} %broadcast_multiply_fusion.10) | copy-start | bytes 12292
  436.3 46.6 %copy-start.70 = (f32[1024]{0:T(1024)}, f32[1024]{0:T(1024)S(1)}, u32[]{:S(2)}) copy-start(f32[1024]{0:T(1024)S(1)} %broadcast_multiply_fusion.8) | copy-start | bytes 12292
  437.8 45.2 %copy-start.80 = (f32[1024]{0:T(1024)}, f32[1024]{0:T(1024)S(1)}, u32[]{:S(2)}) copy-start(f32[1024]{0:T(1024)S(1)} %add_rsqrt_fusion) | copy-start | bytes 12292
  437.8 45.1 %copy-start.82 = (f32[1024]{0:T(1024)}, f32[1024]{0:T(1024)S(1)}, u32[]{:S(2)}) copy-start(f32[1024]{0:T(1024)S(1)} %add_rsqrt_fusion.2) | copy-start | bytes 12292
  455.1 711.9 %reduce-scatter.7.cloned.1.call-start = ((), (), s32[]{:S(2)}) async-start(), calls=%async_computation.7 | async-start | bytes 4718592 | tf_op jit(solution)/shard_map/reduce_scatter | solution.py:243
  793.7 6.9 copy-start.11
  800.6 366.4 %reduce-scatter.5.cloned.1.call-start = ((), (), s32[]{:S(2)}) async-start(), calls=%async_computation.6 | async-start | bytes 4718592 | tf_op jit(solution)/shard_map/reduce_scatter | solution.py:240
  817.2 403.2 %reduce-scatter.11.cloned.1.call-start = ((), (), s32[]{:S(2)}) async-start(), calls=%async_computation.9 | async-start | bytes 4718592 | tf_op jit(solution)/shard_map/reduce_scatter | solution.py:243
  825.3 6.3 copy-start.5
  850.6 6.4 copy-start.6
  863.4 6.3 copy-start.5
  882.3 6.3 copy-start.5
  901.1 6.3 copy-start.5
  920.1 6.3 copy-start.5
  939.2 6.3 copy-start.5
  958.2 6.3 copy-start.5
  977.1 6.3 copy-start.5
  995.9 6.3 copy-start.5
  1014.8 6.3 copy-start.5
  1052.5 6.3 copy-start.5
  1071.3 6.3 copy-start.5
  1124.2 6.8 copy-start.12
  1131.1 181.1 %reduce-scatter.9.cloned.1.call-start = ((), (), s32[]{:S(2)}) async-start(), calls=%async_computation.8 | async-start | bytes 4718592 | tf_op jit(solution)/shard_map/reduce_scatter | solution.py:240
  1144.1 322.5 %all-reduce.10.cloned.1.call-start = ((), (), s32[]{:S(2)}) async-start(), calls=%async_computation.12 | async-start | bytes 6291456 | tf_op jit(solution)/shard_map/psum | solution.py:274
  1167.0 145.2 %copy-start.61 = (f32[1024]{0:T(1024)S(1)}, f32[1024]{0:T(1024)}, u32[]{:S(2)}) copy-start(f32[1024]{0:T(1024)} %copy-done.60) | copy-start | bytes 12292
  1167.0 145.1 %copy-start.79 = (f32[1024]{0:T(1024)S(1)}, f32[1024]{0:T(1024)}, u32[]{:S(2)}) copy-start(f32[1024]{0:T(1024)} %copy-done.78) | copy-start | bytes 12292
  1316.2 181.5 %all-reduce.12.cloned.1.call-start = ((), (), s32[]{:S(2)}) async-start(), calls=%async_computation.13 | async-start | bytes 8388608 | tf_op jit(solution)/shard_map/psum | solution.py:142
  1472.8 24.9 %copy-start.98 = (f32[512]{0:T(512)S(1)}, f32[512]{0:T(512)}, u32[]{:S(2)}) copy-start(f32[512]{0:T(512)} %param.35) | copy-start | bytes 6148
  (232 other events, 855.4 us)
Sparse Core Ops, SparseCore 0:
  14.6 77.6 all-gather.10
  95.1 71.6 all-gather.12
  169.6 71.6 all-gather.6
  243.8 71.6 all-gather.8
  412.0 21.7 all-reduce.15
  455.3 22.4 all-reduce.13
  800.7 89.2 reduce-scatter.6
  894.1 87.8 reduce-scatter.4
  1131.2 89.2 reduce-scatter.10
  1224.3 87.7 reduce-scatter.8
  1318.7 147.7 all-reduce.9
  1470.0 27.6 all-reduce.11
where the time goes:
time: 1570 us
  matrix products  660 us (42%)
  waiting for transfers between devices  337 us (21%)
  local copies, waits for them, and re-layouts  215 us (14%)
  other arithmetic  207 us (13%)
  blocking collectives  107 us (7%)
  loops' own time  23.1 us (1%)
  between operations  15.8 us (1%)
    dot_general x32, matrix products, key_step(): jnp.einsum('qhd,khd->hqk', grad_heads, value_part, preferred_element_type...  148 us
    psum x1, waiting for transfers between devices, on_device(): lax.psum(sums[2].astype(jnp.bfloat16), ('dp', 'seq')).astype(jnp.float32)  135 us
    dot_general x32, matrix products, key_step(): jnp.einsum('hqk,khd->qhd', grad_scores, key_part, preferred_element_type=...  105 us
    dot_general x2, matrix products, on_device(): jnp.einsum('hqk,khd->hqd', weights.astype(jnp.bfloat16), value_part.resha...  102 us
    dot_general x2, matrix products, on_device(): jnp.einsum('qhd,khd->hqk', query_heads, key_part.reshape(row_count, heads...  100 us
    reduce_scatter x2, waiting for transfers between devices, on_device(): lax.psum_scatter(key_terms.astype(jnp.bfloat16), 'seq', scatter_dimension...  91.7 us
    reduce_sum x2, other arithmetic, on_device(): weight_sum = jnp.sum(weights, -1)  87.9 us
    dot_general x32, matrix products, key_step(): jnp.einsum('hqk,qhd->khd', probs.astype(jnp.bfloat16), grad_heads, prefer...  58.4 us
  transfers between devices with their start and end apart: 12, of which 7 were waited for; matrix products, arithmetic and copies ran while one was open for 41% of the time, Pallas kernels for 0%

commit v1 on v0

--- a/solution.py
+++ b/solution.py
@@ -6,6 +6,24 @@
 HEAD_DIM = 64
 EPSILON = 1e-05
 MASKED = -1e30
+
+
+def ring_gather(shard, axis, dim):
+    ways, here, hop = (lax.axis_size(axis), lax.axis_index(axis), shard.shape[dim])
+    shape = [n * ways if d == dim else n for d, n in enumerate(shard.shape)]
+    full = lax.dynamic_update_slice_in_dim(
+        jnp.zeros(shape, shard.dtype), shard, here * hop, axis=dim
+    )
+    going_up = going_down = shard
+    for far in range(1, ways // 2 + 1):
+        going_up = lax.ppermute(going_up, axis, [(d, (d + 1) % ways) for d in range(ways)])
+        full = lax.dynamic_update_slice_in_dim(full, going_up, (here - far) % ways * hop, axis=dim)
+        if 2 * far < ways:
+            going_down = lax.ppermute(going_down, axis, [(d, (d - 1) % ways) for d in range(ways)])
+            full = lax.dynamic_update_slice_in_dim(
+                full, going_down, (here + far) % ways * hop, axis=dim
+            )
+    return full
 
 
 def layer_norm(rows, gain, offset):
@@ -57,7 +75,7 @@
     heads_here = local_width // HEAD_DIM
     score_scale = HEAD_DIM ** (-0.5)
     seg_all, keep_all = (
-        lax.all_gather(segments, "seq", axis=1, tiled=True),
+        ring_gather(segments, "seq", 1),
         lax.all_gather(keep_mask, "seq", axis=1, tiled=True),
     )
     full_length = seg_all.shape[1]

time: 1570 us -> 1570 us (level)
  blocking collectives: 107 us -> 73.9 us
  starting transfers between devices: 1.75 us -> 17.8 us
    all_gather x1 -> x0, blocking collectives: 32.7 us -> none  [on_device(): lax.all_gather(segments, 'seq', axis=1, tiled=True)]
    ppermute x0 -> x7, starting transfers between devices: none -> 16.1 us  [the longest x3 12.5 us: ring_gather(): lax.ppermute(going_down, axis, [(d, (d - 1) % ways) for d in range(ways)])]
  transfers between devices with their start and end apart: 12 -> 19, of which waited for: 7 -> 10; matrix products, arithmetic and copies ran while one was open for 41% -> 41% of each run, Pallas kernels for 0% -> 0%
where the time goes in v1:
time: 1570 us
  matrix products  660 us (42%)
  waiting for transfers between devices  352 us (22%)
  local copies, waits for them, and re-layouts  215 us (14%)
  other arithmetic  207 us (13%)
  blocking collectives  73.9 us (5%)
  loops' own time  22.9 us (1%)
  starting transfers between devices  17.8 us (1%)
  between operations  16 us (1%)
    dot_general x32, matrix products, key_step(): jnp.einsum('qhd,khd->hqk', grad_heads, value_part, preferred_element_type...  148 us
    psum x1, waiting for transfers between devices, on_device(): lax.psum(sums[2].astype(jnp.bfloat16), ('dp', 'seq')).astype(jnp.float32)  135 us
    dot_general x32, matrix products, key_step(): jnp.einsum('hqk,khd->qhd', grad_scores, key_part, preferred_element_type=...  106 us
    dot_general x2, matrix products, on_device(): jnp.einsum('hqk,khd->hqd', weights.astype(jnp.bfloat16), value_part.resha...  102 us
    dot_general x2, matrix products, on_device(): jnp.einsum('qhd,khd->hqk', query_heads, key_part.reshape(row_count, heads...  100 us
    reduce_scatter x2, waiting for transfers between devices, on_device(): lax.psum_scatter(key_terms.astype(jnp.bfloat16), 'seq', scatter_dimension...  91.6 us
    reduce_sum x2, other arithmetic, on_device(): weight_sum = jnp.sum(weights, -1)  88 us
    dot_general x32, matrix products, key_step(): jnp.einsum('hqk,qhd->khd', probs.astype(jnp.bfloat16), grad_heads, prefer...  58.4 us
  transfers between devices with their start and end apart: 19, of which 10 were waited for; matrix products, arithmetic and copies ran while one was open for 41% of the time, Pallas kernels for 0%

profile of v1, /device:TPU:0, one launch (start us, length us, event | category | flops | bytes accessed | tf_op | source)
XLA Modules:
  0.0 1565.2 jit_solution(11156361678083689009)
XLA Ops:
  31.1 30.9 %all_gather.19 = s32[2,8192]{1,0:T(2,128)S(1)} all-gather(s32[2,1024]{1,0:T(2,128)S(1)} %copy-done.89), channel_id=1, replica_groups=mesh['dp'=2,'seq'=8,'tensor'=2] {'seq'}, dimensions={1}, use_global_device_ids=true | all-gather | bytes 73728 | tf_op jit(solution)/shard_map/all_gather | solution.py:79
  64.7 4.7 collective-permute-start.3
  71.2 4.7 collective-permute-start.5
  78.4 6.4 collective-permute-done.6
  84.9 24.5 %fusion.37 = (pred[1024,8192]{1,0:T(8,128)(4,1)}, pred[1024,8192]{1,0:T(8,128)(4,1)}) fusion(s32[8192]{0:T(1024)S(1)} %bitcast.455, s32[1024]{0:T(1024)S(1)} %iota_add_fusion.4, s32[1024]{0:T(1024)S(1)} %bitcast.451, pred[8192]{0:T(1024)(128)(4,1)S(1)} %get-tuple-element.339, pred[8192]{0:T(1024)(128)(4,1)S(1)} %get-tuple-element.338, ...), kind=kLoop, calls=%fused_computation.59 | loop fusion | flops 83886080 | bytes 16871424 | tf_op jit(solution)/shard_map/and | solution.py:52
  109.5 50.0 %fusion.20 = (f32[4,1024]{1,0:T(4,128)S(1)}, f32[4,1024,8192]{2,1,0:T(8,128)}) fusion(pred[1024,8192]{1,0:T(8,128)(4,1)} %get-tuple-element.451, bf16[1024,4,64]{0,2,1:T(8,128)(2,1)S(1)} %get-tuple-element.729, bf16[8192,4,64]{0,2,1:T(8,128)(2,1)} %bitcast.448), kind=kOutput, calls=%fused_computation.42 | convolution fusion | flops 4395626496 | bytes 147341312 | tf_op jit(solution)/shard_map/qhd,khd->hqk/dot_general | solution.py:124
  159.5 7.2 all-gather.13.cloned.1.call-done
  166.6 50.2 %fusion.21 = (f32[4,1024]{1,0:T(4,128)S(1)}, f32[4,1024,8192]{2,1,0:T(8,128)}) fusion(pred[1024,8192]{1,0:T(8,128)(4,1)} %get-tuple-element.450, bf16[1024,4,64]{0,2,1:T(8,128)(2,1)S(1)} %get-tuple-element.672, bf16[8192,4,64]{0,2,1:T(8,128)(2,1)} %bitcast.445), kind=kOutput, calls=%fused_computation.43 | convolution fusion | flops 4395626496 | bytes 147341312 | tf_op jit(solution)/shard_map/qhd,khd->hqk/dot_general | solution.py:124
  217.4 44.0 %fusion.22 = f32[4,1024]{1,0:T(4,128)S(1)} fusion(f32[4,1024,8192]{2,1,0:T(8,128)} %get-tuple-element.459, f32[4,1024]{1,0:T(4,128)S(1)} %broadcast_maximum_fusion.1, pred[1024,8192]{1,0:T(8,128)(4,1)} %get-tuple-element.451), kind=kLoop, calls=%fused_computation.44 | loop fusion | flops 167768064 | bytes 142639104 | tf_op jit(solution)/shard_map/reduce_sum | solution.py:135
  261.5 51.2 %divide_convert_fusion.1 = bf16[1024,4,64]{0,2,1:T(8,128)(2,1)S(1)} fusion(bf16[8192,4,64]{0,2,1:T(8,128)(2,1)} %bitcast.450, f32[4,1024,8192]{2,1,0:T(8,128)} %get-tuple-element.459, f32[4,1024]{1,0:T(4,128)S(1)} %broadcast_maximum_fusion.1, pred[1024,8192]{1,0:T(8,128)(4,1)} %get-tuple-element.451, f32[1024,4]{0,1:T(4,128)S(1)} %bitcast.460), kind=kOutput, calls=%fused_computation.207 | convolution fusion | flops 4463263744 | bytes 147357696 | tf_op jit(solution)/shard_map/hqk,khd->hqd/dot_general | solution.py:136
  314.2 43.9 %fusion.24 = f32[4,1024]{1,0:T(4,128)S(1)} fusion(f32[4,1024,8192]{2,1,0:T(8,128)} %get-tuple-element.461, f32[4,1024]{1,0:T(4,128)S(1)} %broadcast_maximum_fusion, pred[1024,8192]{1,0:T(8,128)(4,1)} %get-tuple-element.450), kind=kLoop, calls=%fused_computation.46 | loop fusion | flops 167768064 | bytes 142639104 | tf_op jit(solution)/shard_map/reduce_sum | solution.py:135
  358.2 51.0 %divide_convert_fusion = bf16[1024,4,64]{0,2,1:T(8,128)(2,1)} fusion(bf16[8192,4,64]{0,2,1:T(8,128)(2,1)} %bitcast.447, f32[4,1024,8192]{2,1,0:T(8,128)} %get-tuple-element.461, f32[4,1024]{1,0:T(4,128)S(1)} %broadcast_maximum_fusion, pred[1024,8192]{1,0:T(8,128)(4,1)} %get-tuple-element.450, f32[1024,4]{0,1:T(4,128)S(1)} %bitcast.459), kind=kOutput, calls=%fused_computation.205 | convolution fusion | flops 4463263744 | bytes 147357696 | tf_op jit(solution)/shard_map/hqk,khd->hqd/dot_general | solution.py:136
  412.1 20.3 %all-reduce.16.cloned.1.call-done = (bf16[1024,512]{1,0:T(8,128)(2,1)}, bf16[1024,512]{1,0:T(8,128)(2,1)}) async-done(((bf16[1024,512]{1,0:T(8,128)(2,1)}, bf16[1024,512]{1,0:T(8,128)(2,1)}), (bf16[1024,512]{1,0:T(8,128)(2,1)}, bf16[1024,512]{1,0:T(8,128)(2,1)})) %all-reduce.16.cloned.1.call-update) | async-done | bytes 2097168 | tf_op jit(solution)/shard_map/psum | solution.py:152
  438.0 5.0 multiply_convert_fusion.5
  456.5 4.6 copy.105
  461.3 15.1 all-reduce.14.cloned.1.call-done
  476.4 5.1 fusion.86
  491.6 300.5 %while.30 = (s32[]{:T(128)}, f32[1024,4,64]{0,2,1:T(8,128)S(1)}, f32[16,512,256]{1,2,0:T(8,128)}, bf16[16,512,256]{1,2,0:T(8,128)(2,1)}, s32[16]{0:T(128)S(1)}, ...) while((s32[]{:T(128)}, f32[1024,4,64]{0,2,1:T(8,128)S(1)}, ...), condition=%wide.region_21.22_spmd.clone, body=%wide.region_20.21_spmd.clone.sunk | while | flops 1366820864 | bytes 135865776 | solution.py:252
  496.9 4.6 fusion.248
  792.1 6.8 copy.56
  799.6 6.7 multiply_convert_fusion.1
  806.3 6.4 copy.55
  820.0 302.8 %while.31 = (s32[]{:T(128)}, f32[1024,4,64]{0,2,1:T(8,128)S(1)}, f32[16,512,256]{1,2,0:T(8,128)}, bf16[16,512,256]{1,2,0:T(8,128)(2,1)}, s32[16]{0:T(128)S(1)}, ...) while((s32[]{:T(128)}, f32[1024,4,64]{0,2,1:T(8,128)S(1)}, ...), condition=%wide.region_32.33_spmd.clone, body=%wide.region_31.32_spmd.clone.sunk | while | flops 1366820864 | bytes 135865776 | solution.py:252
  825.3 4.7 fusion.263
  844.3 4.7 fusion.263
  863.5 4.7 fusion.263
  882.4 4.7 fusion.263
  901.3 4.7 fusion.263
  920.3 4.7 fusion.263
  939.4 4.7 fusion.263
  958.4 4.7 fusion.263
  977.3 4.7 fusion.263
  996.2 4.7 fusion.263
  1015.0 4.7 fusion.263
  1033.9 4.7 fusion.263
  1052.7 4.7 fusion.263
  1071.6 4.7 fusion.263
  1090.4 4.7 fusion.263
  1109.3 4.7 fusion.263
  1122.9 6.8 copy.59
  1129.7 6.6 multiply_convert_fusion
  1136.3 6.4 copy.58
  1169.5 49.4 %reduce-scatter.11.cloned.1.call-done = bf16[1024,256]{1,0:T(8,128)(2,1)} async-done(((bf16[8192,256]{1,0:T(8,128)(2,1)}), bf16[1024,256]{1,0:T(8,128)(2,1)}) %reduce-scatter.11.cloned.1.call-update) | async-done | bytes 524304 | tf_op jit(solution)/shard_map/reduce_scatter | solution.py:261
  1218.9 91.6 %reduce-scatter.9.cloned.1.call-done = bf16[1024,256]{1,0:T(8,128)(2,1)} async-done(((bf16[8192,256]{1,0:T(8,128)(2,1)}), bf16[1024,256]{1,0:T(8,128)(2,1)}) %reduce-scatter.9.cloned.1.call-update) | async-done | bytes 524304 | tf_op jit(solution)/shard_map/reduce_scatter | solution.py:258
  1330.1 134.9 %all-reduce.10.cloned.1.call-done = (bf16[3,512,256]{1,2,0:T(8,128)(2,1)}, bf16[256,512]{1,0:T(8,128)(2,1)}, bf16[512,1024]{1,0:T(8,128)(2,1)}, bf16[1024,512]{1,0:T(8,128)(2,1)}) async-done(((bf16[3,512,256]{1,2,0:T(8,128)(2,1)}, bf16[256,512]{1,0:T(8,128)(2,1)}, bf16[512,1024]{1,0:T(8,128)(2,1)}, bf16[1024,512]{1,0:T(8,128)(2,1)}), (bf16[3,512,256]{1,2,0:T(8,128)(2,1)}, bf16[256,512]{1,0:T(8,128)(2,1)}, ...) | async-done | bytes 3145744 | tf_op jit(solution)/shard_map/psum | solution.py:292
  1472.8 23.3 %all-reduce.12.cloned.1.call-done = (bf16[1024,512]{1,0:T(8,128)(2,1)}, bf16[1024,512]{1,0:T(8,128)(2,1)}, bf16[1024,512]{1,0:T(8,128)(2,1)}, bf16[1024,512]{1,0:T(8,128)(2,1)}) async-done(((bf16[1024,512]{1,0:T(8,128)(2,1)}, bf16[1024,512]{1,0:T(8,128)(2,1)}, bf16[1024,512]{1,0:T(8,128)(2,1)}, bf16[1024,512]{1,0:T(8,128)(2,1)}), (bf16[1024,512]{1,0:T(8,128)(2,1)}, bf16[1024,512]{1,0:T(8,128)(2,1)}, ...) | async-done | bytes 4194320 | tf_op jit(solution)/shard_map/psum | solution.py:160
  1496.1 6.0 fusion.87
  1502.2 42.9 %all-reduce = (bf16[512]{0:T(512)(128)(2,1)S(1)}, bf16[512]{0:T(512)(128)(2,1)S(1)}, bf16[2,256]{1,0:T(2,128)(2,1)S(1)}, bf16[512]{0:T(512)(128)(2,1)S(1)}, bf16...) all-reduce(bf16[512]{0:T(512)(128)(2,1)S(1)} %add_convert_fusion.15, ...), channel_id=1, replica_groups=mesh['dp'=2,'seq'=8,'tensor'=2] {'dp','seq'}, use_global_device_ids=true, to_apply=%region_40.41 | all-reduce | flops 4608 | bytes 18432 | tf_op jit(solution)/shard_map/psum | solution.py:290
  (1114 shorter events, 640.2 us)
Async XLA Ops:
  7.2 429.2 %copy-start = (bf16[512,1024]{1,0:T(8,128)(2,1)S(1)}, bf16[512,1024]{1,0:T(8,128)(2,1)}, u32[]{:S(2)}) copy-start(bf16[512,1024]{1,0:T(8,128)(2,1)} %param.32) | copy-start | bytes 3145732
  7.2 102.2 %all-gather.11.cloned.1.call-start = ((), (), s32[]{:S(2)}) async-start(), calls=%async_computation.10 | async-start | bytes 4718592 | tf_op jit(solution)/shard_map/all_gather | solution.py:116
  14.5 152.2 %all-gather.13.cloned.1.call-start = ((), (), s32[]{:S(2)}) async-start(), calls=%async_computation.11 | async-start | bytes 4718592 | tf_op jit(solution)/shard_map/all_gather | solution.py:116
  19.6 241.9 %all-gather.7.cloned.1.call-start = ((), (), s32[]{:S(2)}) async-start(), calls=%async_computation.4 | async-start | bytes 4718592 | tf_op jit(solution)/shard_map/all_gather | solution.py:117
  22.4 335.8 %all-gather.9.cloned.1.call-start = ((), (), s32[]{:S(2)}) async-start(), calls=%async_computation.5 | async-start | bytes 4718592 | tf_op jit(solution)/shard_map/all_gather | solution.py:117
  22.5 42.1 %collective-permute-start = (s32[2,1024]{1,0:T(2,128)S(1)}, s32[2,1024]{1,0:T(2,128)S(1)}, u32[]{:S(2)}, u32[]{:S(2)}) collective-permute-start(s32[2,1024]{1,0:T(2,128)S(1)} %copy-done.84), channel_id=1, source_target_pairs={{0,2},{2,4},{4,6},{6,8},{8,10},{10,12},{12,14},{14,0},{1,3},{3,5},... | collective-permute-start | bytes 24584 | tf_op jit(solution)/shard_map/ppermute | solution.py:19
  25.5 39.2 %collective-permute-start.1 = (s32[2,1024]{1,0:T(2,128)S(1)}, s32[2,1024]{1,0:T(2,128)S(1)}, u32[]{:S(2)}, u32[]{:S(2)}) collective-permute-start(s32[2,1024]{1,0:T(2,128)S(1)} %copy-done.84), channel_id=1, source_target_pairs={{0,14},{2,0},{4,2},{6,4},{8,6},{10,8},{12,10},{14,12},{1,15},{3,1}... | collective-permute-start | bytes 24584 | tf_op jit(solution)/shard_map/ppermute | solution.py:22
  28.6 403.8 %all-reduce.16.cloned.1.call-start = ((), (), s32[]{:S(2)}) async-start(), calls=%async_computation.15 | async-start | bytes 4194304 | tf_op jit(solution)/shard_map/psum | solution.py:152
  28.7 56.2 %copy-start.54 = (s32[1,1024]{1,0:T(1,128)}, s32[1,1024]{1,0:T(1,128)S(1)}, u32[]{:S(2)}) copy-start(s32[1,1024]{1,0:T(1,128)S(1)} %get-tuple-element.669) | copy-start | bytes 12292
  28.7 56.2 %copy-start.56 = (s32[1,1024]{1,0:T(1,128)}, s32[1,1024]{1,0:T(1,128)S(1)}, u32[]{:S(2)}) copy-start(s32[1,1024]{1,0:T(1,128)S(1)} %get-tuple-element.726) | copy-start | bytes 12292
  28.7 34.3 %slice-start = ((f32[3,1024,256]{1,2,0:T(8,128)}), f32[1,1024,256]{1,2,0:T(8,128)S(1)}, s32[]{:S(2)}) async-start(f32[3,1024,256]{1,2,0:T(8,128)} %copy-done.36), calls=%async_computation.16 | async-start | bytes 2097152 | tf_op jit(solution)/shard_map/slice | solution.py:111
  64.4 45.1 %copy-start.16 = (bf16[1024,4,64]{0,2,1:T(8,128)(2,1)}, bf16[1024,4,64]{0,2,1:T(8,128)(2,1)S(1)}, u32[]{:S(2)}) copy-start(bf16[1024,4,64]{0,2,1:T(8,128)(2,1)S(1)} %get-tuple-element.729) | copy-start | bytes 1572868
  64.4 102.2 %copy-start.14 = (bf16[1024,4,64]{0,2,1:T(8,128)(2,1)}, bf16[1024,4,64]{0,2,1:T(8,128)(2,1)S(1)}, u32[]{:S(2)}) copy-start(bf16[1024,4,64]{0,2,1:T(8,128)(2,1)S(1)} %get-tuple-element.672) | copy-start | bytes 1572868
  64.6 6.6 collective-permute-start.2
  64.7 6.6 collective-permute-start.3
  71.2 6.6 collective-permute-start.4
  71.2 7.1 collective-permute-start.5
  77.8 7.0 collective-permute-start.6
  84.9 24.6 %copy-start.58 = (s32[1,8192]{1,0:T(1,128)}, s32[1,8192]{1,0:T(1,128)S(1)}, u32[]{:S(2)}) copy-start(s32[1,8192]{1,0:T(1,128)S(1)} %get-tuple-element.444) | copy-start | bytes 98308
  84.9 24.6 %copy-start.59 = (s32[1,8192]{1,0:T(1,128)}, s32[1,8192]{1,0:T(1,128)S(1)}, u32[]{:S(2)}) copy-start(s32[1,8192]{1,0:T(1,128)S(1)} %get-tuple-element.445) | copy-start | bytes 98308
  159.4 57.4 %copy-start.68 = (f32[4,1024]{1,0:T(4,128)}, f32[4,1024]{1,0:T(4,128)S(1)}, u32[]{:S(2)}) copy-start(f32[4,1024]{1,0:T(4,128)S(1)} %get-tuple-element.458) | copy-start | bytes 49156
  261.5 51.3 %copy-start.64 = (f32[4,1024]{1,0:T(4,128)}, f32[4,1024]{1,0:T(4,128)S(1)}, u32[]{:S(2)}) copy-start(f32[4,1024]{1,0:T(4,128)S(1)} %fusion.22) | copy-start | bytes 49156
  261.5 51.2 %copy-start.37 = (bf16[256,512]{1,0:T(8,128)(2,1)S(1)}, bf16[256,512]{1,0:T(8,128)(2,1)}, u32[]{:S(2)}) copy-start(bf16[256,512]{1,0:T(8,128)(2,1)} %param.28) | copy-start | bytes 786436
  312.7 45.4 %copy-start.32 = (bf16[1024,4,64]{0,2,1:T(8,128)(2,1)}, bf16[1024,4,64]{0,2,1:T(8,128)(2,1)S(1)}, u32[]{:S(2)}) copy-start(bf16[1024,4,64]{0,2,1:T(8,128)(2,1)S(1)} %divide_convert_fusion.1) | copy-start | bytes 1572868
  409.1 23.2 %copy-start.8 = (bf16[2,1024,512]{2,1,0:T(8,128)(2,1)S(1)}, bf16[2,1024,512]{2,1,0:T(8,128)(2,1)}, u32[]{:S(2)}) copy-start(bf16[2,1024,512]{2,1,0:T(8,128)(2,1)} %param.20) | copy-start | bytes 6291460
  409.2 23.2 %copy-start.74 = (f32[512]{0:T(512)S(1)}, f32[512]{0:T(512)}, u32[]{:S(2)}) copy-start(f32[512]{0:T(512)} %param.29) | copy-start | bytes 6148
  411.8 64.5 %all-reduce.14.cloned.1.call-start = ((), (), s32[]{:S(2)}) async-start(), calls=%async_computation.14 | async-start | bytes 4194304 | tf_op jit(solution)/shard_map/psum | solution.py:174
  434.9 46.6 %copy-start.72 = (f32[1024]{0:T(1024)}, f32[1024]{0:T(1024)S(1)}, u32[]{:S(2)}) copy-start(f32[1024]{0:T(1024)S(1)} %broadcast_multiply_fusion.10) | copy-start | bytes 12292
  434.9 46.6 %copy-start.70 = (f32[1024]{0:T(1024)}, f32[1024]{0:T(1024)S(1)}, u32[]{:S(2)}) copy-start(f32[1024]{0:T(1024)S(1)} %broadcast_multiply_fusion.8) | copy-start | bytes 12292
  436.4 45.2 %copy-start.80 = (f32[1024]{0:T(1024)}, f32[1024]{0:T(1024)S(1)}, u32[]{:S(2)}) copy-start(f32[1024]{0:T(1024)S(1)} %add_rsqrt_fusion) | copy-start | bytes 12292
  436.4 45.1 %copy-start.82 = (f32[1024]{0:T(1024)}, f32[1024]{0:T(1024)S(1)}, u32[]{:S(2)}) copy-start(f32[1024]{0:T(1024)S(1)} %add_rsqrt_fusion.2) | copy-start | bytes 12292
  453.7 712.0 %reduce-scatter.7.cloned.1.call-start = ((), (), s32[]{:S(2)}) async-start(), calls=%async_computation.7 | async-start | bytes 4718592 | tf_op jit(solution)/shard_map/reduce_scatter | solution.py:261
  792.1 6.8 copy-start.11
  798.9 366.8 %reduce-scatter.5.cloned.1.call-start = ((), (), s32[]{:S(2)}) async-start(), calls=%async_computation.6 | async-start | bytes 4718592 | tf_op jit(solution)/shard_map/reduce_scatter | solution.py:258
  806.3 6.4 copy-start.34
  806.3 6.4 copy-start.38
  815.6 403.3 %reduce-scatter.11.cloned.1.call-start = ((), (), s32[]{:S(2)}) async-start(), calls=%async_computation.9 | async-start | bytes 4718592 | tf_op jit(solution)/shard_map/reduce_scatter | solution.py:261
  849.0 6.4 copy-start.6
  918.7 6.3 copy-start.5
  1013.4 6.3 copy-start.5
  1107.6 6.3 copy-start.5
  1122.9 6.8 copy-start.12
  1129.7 180.8 %reduce-scatter.9.cloned.1.call-start = ((), (), s32[]{:S(2)}) async-start(), calls=%async_computation.8 | async-start | bytes 4718592 | tf_op jit(solution)/shard_map/reduce_scatter | solution.py:258
  1142.7 322.2 %all-reduce.10.cloned.1.call-start = ((), (), s32[]{:S(2)}) async-start(), calls=%async_computation.12 | async-start | bytes 6291456 | tf_op jit(solution)/shard_map/psum | solution.py:292
  1165.7 144.8 %copy-start.61 = (f32[1024]{0:T(1024)S(1)}, f32[1024]{0:T(1024)}, u32[]{:S(2)}) copy-start(f32[1024]{0:T(1024)} %copy-done.60) | copy-start | bytes 12292
  1165.7 144.8 %copy-start.79 = (f32[1024]{0:T(1024)S(1)}, f32[1024]{0:T(1024)}, u32[]{:S(2)}) copy-start(f32[1024]{0:T(1024)} %copy-done.78) | copy-start | bytes 12292
  1314.5 181.6 %all-reduce.12.cloned.1.call-start = ((), (), s32[]{:S(2)}) async-start(), calls=%async_computation.13 | async-start | bytes 8388608 | tf_op jit(solution)/shard_map/psum | solution.py:160
  1471.2 24.9 %copy-start.98 = (f32[512]{0:T(512)S(1)}, f32[512]{0:T(512)}, u32[]{:S(2)}) copy-start(f32[512]{0:T(512)} %param.35) | copy-start | bytes 6148
  (239 other events, 899.1 us)
Sparse Core Ops, SparseCore 0:
  14.6 77.4 all-gather.10
  94.8 71.7 all-gather.12
  169.4 71.6 all-gather.6
  243.7 71.6 all-gather.8
  411.9 20.4 all-reduce.15
  453.8 22.4 all-reduce.13
  799.0 89.2 reduce-scatter.6
  892.4 87.8 reduce-scatter.4
  1129.8 89.0 reduce-scatter.10
  1222.8 87.6 reduce-scatter.8
  1317.0 147.8 all-reduce.9
  1468.4 27.6 all-reduce.11
